TPU v7x, 128 devices: a whole 4x4x4 slice. The times are simulated.
128 devices in a mesh: mic: 8 (over x_lo, z), tm: 16 (over x_hi, y, core).
Axes of the slice: x: 4 (x_hi: 2, x_lo: 2; x = x_hi * 2 + x_lo), y: 4, z: 4, core: 2. Of those that a mesh axis runs over, the one named last changes fastest.
Arguments:
- signal: float32 [8, 16384, 512], P('mic', 'tm'), may hold values from -6 to 6
- conv_weight: float32 [2, 3, 2, 512, 512], replicated, may hold values from -0.1875 to 0.1875
- conv_bias: float32 [2, 3, 512], replicated, may hold values from -3 to 3
- transform_in: float32 [2, 512, 512], replicated, may hold values from -0.25 to 0.25
- transform_mid: float32 [2, 512, 512], replicated, may hold values from -0.25 to 0.25
- transform_out: float32 [2, 1024, 512], replicated, may hold values from -0.1875 to 0.1875
- transform_offsets_bias: float32 [2, 3, 512], replicated, may hold values from -3 to 3
Outputs:
- separated: float32 [8, 16384, 512], P('mic', 'tm')
All inputs are finite; a program needn't handle non-finite values.
Results may differ from a plain program's by a relative error of at most 0.0001.
Values sent between devices are 32-bit elements; how exact they have to be, the bound alone decides.
No kernel may reach another device: no remote copies, remote signals or barrier semaphores. Data moves between devices by JAX's collectives and lax.ppermute only.
A program may use at most 128 MiB of HBM per device.

v0:
```python
import jax
import jax.numpy as jnp
from jax import lax
from jax.sharding import PartitionSpec as P

SEPARATOR_BLOCKS = 2


def from_behind(x, axis, by):
    length = lax.axis_size(axis)
    pairs = [(i, i + by) for i in range(length) if 0 <= i + by < length]
    return lax.ppermute(x, axis, pairs)


def matmul(left, right):
    return jnp.dot(left, right, precision=lax.Precision.HIGHEST, preferred_element_type=jnp.float32)


def convolve(hidden_activations, weights, bias, delayed):
    return hidden_activations + jnp.tanh(
        matmul(hidden_activations, weights[0]) + matmul(delayed, weights[1]) + bias
    )


def body(
    signal,
    conv_weight,
    conv_bias,
    transform_in,
    transform_mid,
    transform_out,
    transform_offsets_bias,
):
    hidden_activations = signal[0]
    frames = hidden_activations.shape[0]
    half = frames // 2
    channels = hidden_activations.shape[1]
    micro_count = jnp.float32(lax.axis_size("mic") * signal.shape[0])
    for section_index in range(SEPARATOR_BLOCKS):
        earlier = from_behind(hidden_activations, "tm", 1)[frames - half :]
        delayed = jnp.concatenate([earlier, hidden_activations[: frames - half]], axis=0)
        hidden_activations = convolve(
            hidden_activations, conv_weight[section_index, 0], conv_bias[section_index, 0], delayed
        )
        delayed = from_behind(hidden_activations, "tm", 1)
        hidden_activations = convolve(
            hidden_activations, conv_weight[section_index, 1], conv_bias[section_index, 1], delayed
        )
        delayed = from_behind(hidden_activations, "tm", 2)
        hidden_activations = convolve(
            hidden_activations, conv_weight[section_index, 2], conv_bias[section_index, 2], delayed
        )
        mapped = jnp.tanh(
            matmul(hidden_activations, transform_in[section_index])
            + transform_offsets_bias[section_index, 0]
        )
        summed = lax.psum(mapped, "mic")
        pooled = jnp.tanh(
            matmul(summed / micro_count, transform_mid[section_index])
            + transform_offsets_bias[section_index, 1]
        )
        mixing = (
            matmul(mapped, transform_out[section_index, :channels])
            + matmul(pooled, transform_out[section_index, channels:])
            + transform_offsets_bias[section_index, 2]
        )
        hidden_activations = hidden_activations + jnp.tanh(mixing)
    return hidden_activations[None]


def solution(mesh):
    placed = (P("mic", "tm", None), P(), P(), P(), P(), P(), P())
    return jax.shard_map(
        body, mesh=mesh, in_specs=placed, out_specs=P("mic", "tm", None), check_vma=False
    )
```

profile of v0, /device:TPU:0, one launch (start us, length us, event | category | flops | bytes accessed | tf_op | source)
XLA Modules:
  0.0 462.4 jit_solution(18367661636955650479)
XLA Ops:
  6.5 0.0 copy-start.2
  6.5 0.0 all-reduce.3.cloned.1.call-start
  6.5 1.5 collective-permute-start
  8.1 0.8 fusion.78
  8.9 1.3 slice_bitcast_fusion
  10.2 0.0 copy-done.2
  10.2 4.7 %fusion.46 = f32[1024,512]{1,0:T(8,128)S(1)} fusion(f32[2,3,2,512,512]{4,3,2,1,0:T(8,128)} %param.8, f32[1,1024,512]{2,1,0:T(8,128)S(1)} %copy-done.2), kind=kOutput, calls=%fused_computation.52 | convolution fusion | flops 3221225472 | bytes 5242880 | tf_op jit(solution)/shard_map/dot_general | solution.py:16
  14.9 0.0 collective-permute-done
  14.9 0.1 slice.178
  15.0 4.9 %tanh_add_fusion.6 = f32[1024,512]{1,0:T(8,128)S(1)} fusion(f32[1024,512]{1,0:T(8,128)S(1)} %fusion.46, f32[512,512]{1,0:T(8,128)S(1)} %slice_bitcast_fusion, f32[512,512]{1,0:T(8,128)S(1)} %slice.178, f32[512]{0:T(512)S(1)} %bitcast.105, f32[2,3,2,512,512]{4,3,2,1,0:T(8,128)} %param.8, f32[1,1024,512]{2,1,0:T(8,128)S(1)} %copy-done.2), kind=kOutput, calls=%fused_computation.27 | convolution fusion | flops 3223322624 | bytes 9439232 | tf_op jit(solution)/shard_map/dot_general | solution.py:16
  19.9 21.0 %collective-permute-start.1 = (f32[1024,512]{1,0:T(8,128)S(1)}, f32[1024,512]{1,0:T(8,128)S(1)}, u32[]{:S(2)}, u32[]{:S(2)}) collective-permute-start(f32[1024,512]{1,0:T(8,128)S(1)} %tanh_add_fusion.6), channel_id=1, source_target_pairs={{0,1},{1,2},{2,3},{3,4},{4,5},{5,6},{6,7},{7,8},{8,9},{9,10},{10,1... | collective-permute-start | bytes 6291464 | tf_op jit(solution)/shard_map/ppermute | solution.py:12
  40.9 4.7 %fusion.43 = f32[1024,512]{1,0:T(8,128)S(1)} fusion(f32[1024,512]{1,0:T(8,128)S(1)} %tanh_add_fusion.6, f32[2,3,2,512,512]{4,3,2,1,0:T(8,128)} %param.8), kind=kOutput, calls=%fused_computation.49 | convolution fusion | flops 3221225472 | bytes 5242880 | tf_op jit(solution)/shard_map/dot_general | solution.py:16
  45.6 0.0 collective-permute-done.1
  45.6 0.0 copy-start.7
  45.7 4.9 %tanh_add_fusion.5 = f32[1024,512]{1,0:T(8,128)S(1)} fusion(f32[1024,512]{1,0:T(8,128)S(1)} %tanh_add_fusion.6, f32[1024,512]{1,0:T(8,128)S(1)} %fusion.43, f32[1024,512]{1,0:T(8,128)S(1)} %collective-permute-done.1, f32[512]{0:T(512)S(1)} %bitcast.103, f32[2,3,2,512,512]{4,3,2,1,0:T(8,128)} %param.8), kind=kOutput, calls=%fused_computation.26 | convolution fusion | flops 3222798336 | bytes 9439232 | tf_op jit(solution)/shard_map/dot_general | solution.py:16
  50.6 24.9 %collective-permute-start.2 = (f32[1024,512]{1,0:T(8,128)S(1)}, f32[1024,512]{1,0:T(8,128)S(1)}, u32[]{:S(2)}, u32[]{:S(2)}) collective-permute-start(f32[1024,512]{1,0:T(8,128)S(1)} %tanh_add_fusion.5), channel_id=1, source_target_pairs={{0,2},{1,3},{2,4},{3,5},{4,6},{5,7},{6,8},{7,9},{8,10},{9,11},{10,... | collective-permute-start | bytes 6291464 | tf_op jit(solution)/shard_map/ppermute | solution.py:12
  75.6 0.0 copy-done.7
  75.6 4.7 %fusion.40 = f32[1024,512]{1,0:T(8,128)S(1)} fusion(f32[1024,512]{1,0:T(8,128)S(1)} %tanh_add_fusion.5, f32[2,3,2,512,512]{4,3,2,1,0:T(8,128)} %param.8), kind=kOutput, calls=%fused_computation.46 | convolution fusion | flops 3221225472 | bytes 5242880 | tf_op jit(solution)/shard_map/dot_general | solution.py:16
  80.3 39.1 %collective-permute-done.2 = f32[1024,512]{1,0:T(8,128)S(1)} collective-permute-done((f32[1024,512]{1,0:T(8,128)S(1)}, f32[1024,512]{1,0:T(8,128)S(1)}, u32[]{:S(2)}, u32[]{:S(2)}) %collective-permute-start.2) | collective-permute-done | bytes 2097184 | tf_op jit(solution)/shard_map/ppermute | solution.py:12
  119.4 0.0 copy-start.5
  119.4 5.1 %tanh_add_fusion.4 = f32[1024,512]{1,0:T(8,128)S(1)} fusion(f32[1024,512]{1,0:T(8,128)S(1)} %tanh_add_fusion.5, f32[1024,512]{1,0:T(8,128)S(1)} %fusion.40, f32[1024,512]{1,0:T(8,128)S(1)} %collective-permute-done.2, f32[512]{0:T(512)S(1)} %bitcast.100, f32[2,3,2,512,512]{4,3,2,1,0:T(8,128)} %param.8), kind=kOutput, calls=%fused_computation.25 | convolution fusion | flops 3222798336 | bytes 9439232 | tf_op jit(solution)/shard_map/dot_general | solution.py:16
  124.5 0.0 copy-done.5
  124.5 4.8 %add_tanh_fusion.1 = f32[1024,512]{1,0:T(8,128)} fusion(f32[1024,512]{1,0:T(8,128)S(1)} %tanh_add_fusion.4, f32[512]{0:T(512)S(1)} %bitcast.104, f32[2,512,512]{2,1,0:T(8,128)S(1)} %copy-done.5), kind=kOutput, calls=%fused_computation.24 | convolution fusion | flops 3221749760 | bytes 5244928 | tf_op jit(solution)/shard_map/dot_general | solution.py:16
  129.3 0.0 all-reduce.3.cloned.1.call-update
  129.3 0.5 all-reduce.5.cloned.1.call-start
  129.8 88.7 %all-reduce.3.cloned.1.call-done = f32[1024,512]{1,0:T(8,128)} async-done(((f32[1024,512]{1,0:T(8,128)}), f32[1024,512]{1,0:T(8,128)}) %all-reduce.3.cloned.1.call-update) | async-done | bytes 2097168 | tf_op jit(solution)/shard_map/psum | solution.py:57
  218.5 0.0 copy-start.3
  218.5 5.5 %fusion.16 = f32[1024,512]{1,0:T(8,128)S(1)} fusion(f32[1024,512]{1,0:T(8,128)} %all-reduce.3.cloned.1.call-done, f32[2,512,512]{2,1,0:T(8,128)} %param.11), kind=kOutput, calls=%fused_computation.22 | convolution fusion | flops 3221749760 | bytes 5242880 | tf_op jit(solution)/shard_map/dot_general | solution.py:16
  224.0 0.0 copy-done.3
  224.0 0.0 copy-start
  224.0 3.6 fusion.13
  227.6 0.0 copy-done
  227.6 3.7 tanh_add_fusion.3
  231.3 1.6 collective-permute-start.3
  232.9 0.1 slice.180
  233.0 4.7 %fusion.33 = f32[1024,512]{1,0:T(8,128)S(1)} fusion(f32[1024,512]{1,0:T(8,128)S(1)} %tanh_add_fusion.3, f32[2,3,2,512,512]{4,3,2,1,0:T(8,128)} %param.8), kind=kOutput, calls=%fused_computation.39 | convolution fusion | flops 3221225472 | bytes 5242880 | tf_op jit(solution)/shard_map/dot_general | solution.py:16
  237.7 0.0 collective-permute-done.3
  237.7 0.1 slice.179
  237.8 5.0 %tanh_add_fusion.2 = f32[1024,512]{1,0:T(8,128)S(1)} fusion(f32[1024,512]{1,0:T(8,128)S(1)} %tanh_add_fusion.3, f32[1024,512]{1,0:T(8,128)S(1)} %fusion.33, f32[512,512]{1,0:T(8,128)S(1)} %slice.180, f32[512,512]{1,0:T(8,128)S(1)} %slice.179, f32[512]{0:T(512)S(1)} %bitcast.98, f32[2,3,2,512,512]{4,3,2,1,0:T(8,128)} %param.8), kind=kOutput, calls=%fused_computation.17 | convolution fusion | flops 3223322624 | bytes 9439232 | tf_op jit(solution)/shard_map/dot_general | solution.py:16
  242.8 22.1 %collective-permute-start.4 = (f32[1024,512]{1,0:T(8,128)S(1)}, f32[1024,512]{1,0:T(8,128)S(1)}, u32[]{:S(2)}, u32[]{:S(2)}) collective-permute-start(f32[1024,512]{1,0:T(8,128)S(1)} %tanh_add_fusion.2), channel_id=1, source_target_pairs={{0,1},{1,2},{2,3},{3,4},{4,5},{5,6},{6,7},{7,8},{8,9},{9,10},{10,1... | collective-permute-start | bytes 6291464 | tf_op jit(solution)/shard_map/ppermute | solution.py:12
  264.9 4.7 %fusion.30 = f32[1024,512]{1,0:T(8,128)S(1)} fusion(f32[1024,512]{1,0:T(8,128)S(1)} %tanh_add_fusion.2, f32[2,3,2,512,512]{4,3,2,1,0:T(8,128)} %param.8), kind=kOutput, calls=%fused_computation.36 | convolution fusion | flops 3221225472 | bytes 5242880 | tf_op jit(solution)/shard_map/dot_general | solution.py:16
  269.6 0.0 collective-permute-done.4
  269.6 4.9 %tanh_add_fusion.1 = f32[1024,512]{1,0:T(8,128)S(1)} fusion(f32[1024,512]{1,0:T(8,128)S(1)} %tanh_add_fusion.2, f32[1024,512]{1,0:T(8,128)S(1)} %fusion.30, f32[1024,512]{1,0:T(8,128)S(1)} %collective-permute-done.4, f32[512]{0:T(512)S(1)} %bitcast.95, f32[2,3,2,512,512]{4,3,2,1,0:T(8,128)} %param.8), kind=kOutput, calls=%fused_computation.16 | convolution fusion | flops 3222798336 | bytes 9439232 | tf_op jit(solution)/shard_map/dot_general | solution.py:16
  274.6 25.2 %collective-permute-start.5 = (f32[1024,512]{1,0:T(8,128)S(1)}, f32[1024,512]{1,0:T(8,128)S(1)}, u32[]{:S(2)}, u32[]{:S(2)}) collective-permute-start(f32[1024,512]{1,0:T(8,128)S(1)} %tanh_add_fusion.1), channel_id=1, source_target_pairs={{0,2},{1,3},{2,4},{3,5},{4,6},{5,7},{6,8},{7,9},{8,10},{9,11},{10,... | collective-permute-start | bytes 6291464 | tf_op jit(solution)/shard_map/ppermute | solution.py:12
  299.8 4.7 %fusion.27 = f32[1024,512]{1,0:T(8,128)S(1)} fusion(f32[1024,512]{1,0:T(8,128)S(1)} %tanh_add_fusion.1, f32[2,3,2,512,512]{4,3,2,1,0:T(8,128)} %param.8), kind=kOutput, calls=%fused_computation.33 | convolution fusion | flops 3221225472 | bytes 5242880 | tf_op jit(solution)/shard_map/dot_general | solution.py:16
  304.5 39.1 %collective-permute-done.5 = f32[1024,512]{1,0:T(8,128)S(1)} collective-permute-done((f32[1024,512]{1,0:T(8,128)S(1)}, f32[1024,512]{1,0:T(8,128)S(1)}, u32[]{:S(2)}, u32[]{:S(2)}) %collective-permute-start.5) | collective-permute-done | bytes 2097184 | tf_op jit(solution)/shard_map/ppermute | solution.py:12
  343.6 0.0 copy-start.6
  343.6 5.1 %tanh_add_fusion = f32[1024,512]{1,0:T(8,128)S(1)} fusion(f32[1024,512]{1,0:T(8,128)S(1)} %tanh_add_fusion.1, f32[1024,512]{1,0:T(8,128)S(1)} %fusion.27, f32[1024,512]{1,0:T(8,128)S(1)} %collective-permute-done.5, f32[512]{0:T(512)S(1)} %bitcast.94, f32[2,3,2,512,512]{4,3,2,1,0:T(8,128)} %param.8), kind=kOutput, calls=%fused_computation.15 | convolution fusion | flops 3222798336 | bytes 9439232 | tf_op jit(solution)/shard_map/dot_general | solution.py:16
  348.7 0.0 copy-done.6
  348.7 4.8 %add_tanh_fusion = f32[1024,512]{1,0:T(8,128)} fusion(f32[1024,512]{1,0:T(8,128)S(1)} %tanh_add_fusion, f32[512]{0:T(512)S(1)} %bitcast.99, f32[2,512,512]{2,1,0:T(8,128)S(1)} %copy-done.6), kind=kOutput, calls=%fused_computation.14 | convolution fusion | flops 3221749760 | bytes 5244928 | tf_op jit(solution)/shard_map/dot_general | solution.py:16
  353.5 0.0 all-reduce.5.cloned.1.call-update
  353.5 87.3 %all-reduce.5.cloned.1.call-done = f32[1024,512]{1,0:T(8,128)} async-done(((f32[1024,512]{1,0:T(8,128)}), f32[1024,512]{1,0:T(8,128)}) %all-reduce.5.cloned.1.call-update) | async-done | bytes 2097168 | tf_op jit(solution)/shard_map/psum | solution.py:57
  440.8 0.0 copy-start.4
  440.8 5.7 %fusion.11 = f32[1024,512]{1,0:T(8,128)S(1)} fusion(f32[1024,512]{1,0:T(8,128)} %all-reduce.5.cloned.1.call-done, f32[2,512,512]{2,1,0:T(8,128)} %param.11), kind=kOutput, calls=%fused_computation.12 | convolution fusion | flops 3221749760 | bytes 5242880 | tf_op jit(solution)/shard_map/dot_general | solution.py:16
  446.5 0.0 copy-done.4
  446.5 0.0 copy-start.1
  446.5 3.5 fusion.8
  450.1 0.0 copy-done.1
  450.1 5.0 %add_bitcast_fusion = f32[1,1024,512]{2,1,0:T(8,128)} fusion(f32[1024,512]{1,0:T(8,128)S(1)} %tanh_add_fusion, f32[1024,512]{1,0:T(8,128)S(1)} %fusion.8, f32[1024,512]{1,0:T(8,128)S(1)} %copy-done.1, f32[512]{0:T(512)S(1)} %bitcast.96, f32[2,1024,512]{2,1,0:T(8,128)S(1)} %copy-done.4), kind=kOutput, calls=%fused_computation.8 | convolution fusion | flops 3222798336 | bytes 9439232 | tf_op jit(solution)/shard_map/dot_general | solution.py:16
  (1 shorter events, 0.0 us)
Async XLA Ops:
  6.5 3.6 copy-start.2
  6.5 212.0 %all-reduce.3.cloned.1.call-start = ((), (), s32[]{:S(2)}) async-start(), calls=%async_computation | async-start | bytes 4194304 | tf_op jit(solution)/shard_map/psum | solution.py:57
  6.5 8.3 %collective-permute-start = (f32[1024,512]{1,0:T(8,128)}, f32[1024,512]{1,0:T(8,128)S(1)}, u32[]{:S(2)}, u32[]{:S(2)}) collective-permute-start(f32[1024,512]{1,0:T(8,128)} %bitcast.93), channel_id=1, source_target_pairs={{0,1},{1,2},{2,3},{3,4},{4,5},{5,6},{6,7},{7,8},{8,9},{9,10},{10,1... | collective-permute-start | bytes 6291464 | tf_op jit(solution)/shard_map/ppermute | solution.py:12
  19.9 25.7 %collective-permute-start.1 = (f32[1024,512]{1,0:T(8,128)S(1)}, f32[1024,512]{1,0:T(8,128)S(1)}, u32[]{:S(2)}, u32[]{:S(2)}) collective-permute-start(f32[1024,512]{1,0:T(8,128)S(1)} %tanh_add_fusion.6), channel_id=1, source_target_pairs={{0,1},{1,2},{2,3},{3,4},{4,5},{5,6},{6,7},{7,8},{8,9},{9,10},{10,1... | collective-permute-start | bytes 6291464 | tf_op jit(solution)/shard_map/ppermute | solution.py:12
  45.6 29.9 %copy-start.7 = (f32[2,3,512]{2,0,1:T(2,128)S(1)}, f32[2,3,512]{2,0,1:T(2,128)}, u32[]{:S(2)}) copy-start(f32[2,3,512]{2,0,1:T(2,128)} %param.13) | copy-start | bytes 36868
  50.6 68.8 %collective-permute-start.2 = (f32[1024,512]{1,0:T(8,128)S(1)}, f32[1024,512]{1,0:T(8,128)S(1)}, u32[]{:S(2)}, u32[]{:S(2)}) collective-permute-start(f32[1024,512]{1,0:T(8,128)S(1)} %tanh_add_fusion.5), channel_id=1, source_target_pairs={{0,2},{1,3},{2,4},{3,5},{4,6},{5,7},{6,8},{7,9},{8,10},{9,11},{10,... | collective-permute-start | bytes 6291464 | tf_op jit(solution)/shard_map/ppermute | solution.py:12
  119.4 5.1 %copy-start.5 = (f32[2,512,512]{2,1,0:T(8,128)S(1)}, f32[2,512,512]{2,1,0:T(8,128)}, u32[]{:S(2)}) copy-start(f32[2,512,512]{2,1,0:T(8,128)} %param.10) | copy-start | bytes 6291460
  129.3 311.5 %all-reduce.5.cloned.1.call-start = ((), (), s32[]{:S(2)}) async-start(), calls=%async_computation.1 | async-start | bytes 4194304 | tf_op jit(solution)/shard_map/psum | solution.py:57
  218.5 5.5 %copy-start.3 = (f32[2,1024,512]{2,1,0:T(8,128)S(1)}, f32[2,1024,512]{2,1,0:T(8,128)}, u32[]{:S(2)}) copy-start(f32[2,1024,512]{2,1,0:T(8,128)} %param.12) | copy-start | bytes 12582916
  224.0 3.6 copy-start
  231.3 6.4 %collective-permute-start.3 = (f32[1024,512]{1,0:T(8,128)S(1)}, f32[1024,512]{1,0:T(8,128)S(1)}, u32[]{:S(2)}, u32[]{:S(2)}) collective-permute-start(f32[1024,512]{1,0:T(8,128)S(1)} %tanh_add_fusion.3), channel_id=1, source_target_pairs={{0,1},{1,2},{2,3},{3,4},{4,5},{5,6},{6,7},{7,8},{8,9},{9,10},{10,1... | collective-permute-start | bytes 6291464 | tf_op jit(solution)/shard_map/ppermute | solution.py:12
  242.8 26.8 %collective-permute-start.4 = (f32[1024,512]{1,0:T(8,128)S(1)}, f32[1024,512]{1,0:T(8,128)S(1)}, u32[]{:S(2)}, u32[]{:S(2)}) collective-permute-start(f32[1024,512]{1,0:T(8,128)S(1)} %tanh_add_fusion.2), channel_id=1, source_target_pairs={{0,1},{1,2},{2,3},{3,4},{4,5},{5,6},{6,7},{7,8},{8,9},{9,10},{10,1... | collective-permute-start | bytes 6291464 | tf_op jit(solution)/shard_map/ppermute | solution.py:12
  274.6 69.0 %collective-permute-start.5 = (f32[1024,512]{1,0:T(8,128)S(1)}, f32[1024,512]{1,0:T(8,128)S(1)}, u32[]{:S(2)}, u32[]{:S(2)}) collective-permute-start(f32[1024,512]{1,0:T(8,128)S(1)} %tanh_add_fusion.1), channel_id=1, source_target_pairs={{0,2},{1,3},{2,4},{3,5},{4,6},{5,7},{6,8},{7,9},{8,10},{9,11},{10,... | collective-permute-start | bytes 6291464 | tf_op jit(solution)/shard_map/ppermute | solution.py:12
  343.6 5.1 %copy-start.6 = (f32[2,512,512]{2,1,0:T(8,128)S(1)}, f32[2,512,512]{2,1,0:T(8,128)}, u32[]{:S(2)}) copy-start(f32[2,512,512]{2,1,0:T(8,128)} %param.10) | copy-start | bytes 6291460
  440.8 5.8 %copy-start.4 = (f32[2,1024,512]{2,1,0:T(8,128)S(1)}, f32[2,1024,512]{2,1,0:T(8,128)}, u32[]{:S(2)}) copy-start(f32[2,1024,512]{2,1,0:T(8,128)} %param.12) | copy-start | bytes 12582916
  446.5 3.5 copy-start.1
Sparse Core Ops, SparseCore 0:
  129.4 89.0 all-reduce.2
  353.6 87.1 all-reduce.4
where the time goes:
time: 469 us; the launch traced here: 462 us
  waiting for transfers between devices  254 us (54%)
  starting transfers between devices  96.9 us (21%)
  matrix products  94.6 us (20%)
  between operations  14.2 us (3%)
    psum x2, waiting for transfers between devices, body(): summed = lax.psum(mapped, 'mic')  176 us
    ppermute x6, starting transfers between devices, from_behind(): return lax.ppermute(x, axis, pairs)  96.4 us
    dot_general x20, matrix products, matmul(): jnp.dot(left, right, precision=lax.Precision.HIGHEST, preferred_element_t...  94.6 us
    ppermute x6, waiting for transfers between devices, from_behind(): return lax.ppermute(x, axis, pairs)  78.2 us
  transfers between devices with their start and end apart: 8, of which 4 were waited for; matrix products, arithmetic and copies ran while one was open for 7% of the time, Pallas kernels for 0%

commit v1 on v0

--- a/solution.py
+++ b/solution.py
@@ -54,7 +54,8 @@
             matmul(hidden_activations, transform_in[section_index])
             + transform_offsets_bias[section_index, 0]
         )
-        summed = lax.psum(mapped, "mic")
+        blocks = lax.all_gather(mapped, "mic", axis=0, tiled=False)
+        summed = blocks.sum(axis=0)
         pooled = jnp.tanh(
             matmul(summed / micro_count, transform_mid[section_index])
             + transform_offsets_bias[section_index, 1]

time: 469 us -> 663 us (1.41)
  waiting for transfers between devices: 254 us -> 429 us
  other arithmetic: 0 us -> 19.1 us
    all_gather x0 -> x2, waiting for transfers between devices: none -> 351 us  [body(): blocks = lax.all_gather(mapped, 'mic', axis=0, tiled=False)]
    psum x2 -> x0, waiting for transfers between devices: 176 us -> none  [body(): summed = lax.psum(mapped, 'mic')]
    reduce_sum x0 -> x2, other arithmetic: none -> 19.1 us  [body(): summed = blocks.sum(axis=0)]
  transfers between devices with their start and end apart: 8 -> 8, of which waited for: 4 -> 4; matrix products, arithmetic and copies ran while one was open for 7% -> 5% of each run, Pallas kernels for 0% -> 0%
where the time goes in v1:
time: 663 us; the launch traced here: 656 us
  waiting for transfers between devices  429 us (65%)
  starting transfers between devices  96.8 us (15%)
  matrix products  94.4 us (14%)
  other arithmetic  19.1 us (3%)
  between operations  14.2 us (2%)
    all_gather x2, waiting for transfers between devices, body(): blocks = lax.all_gather(mapped, 'mic', axis=0, tiled=False)  351 us
    ppermute x6, starting transfers between devices, from_behind(): return lax.ppermute(x, axis, pairs)  96.4 us
    dot_general x20, matrix products, matmul(): jnp.dot(left, right, precision=lax.Precision.HIGHEST, preferred_element_t...  94.4 us
    ppermute x6, waiting for transfers between devices, from_behind(): return lax.ppermute(x, axis, pairs)  78.3 us
    reduce_sum x2, other arithmetic, body(): summed = blocks.sum(axis=0)  19.1 us
  transfers between devices with their start and end apart: 8, of which 4 were waited for; matrix products, arithmetic and copies ran while one was open for 5% of the time, Pallas kernels for 0%

profile of v1, /device:TPU:0, one launch (start us, length us, event | category | flops | bytes accessed | tf_op | source)
XLA Modules:
  0.0 656.2 jit_solution(14769996941360824176)
XLA Ops:
  6.5 0.0 copy-start.2
  6.5 0.0 all-gather.5.cloned.1.call-start
  6.5 1.5 collective-permute-start
  8.1 0.8 fusion.78
  8.9 1.3 slice_bitcast_fusion
  10.2 0.0 copy-done.2
  10.2 4.7 fusion.46
  14.9 0.0 collective-permute-done
  14.9 0.1 slice.178
  15.0 4.9 tanh_add_fusion.6
  19.9 21.0 %collective-permute-start.1 = (f32[1024,512]{1,0:T(8,128)S(1)}, f32[1024,512]{1,0:T(8,128)S(1)}, u32[]{:S(2)}, u32[]{:S(2)}) collective-permute-start(f32[1024,512]{1,0:T(8,128)S(1)} %tanh_add_fusion.6), channel_id=1, source_target_pairs={{0,1},{1,2},{2,3},{3,4},{4,5},{5,6},{6,7},{7,8},{8,9},{9,10},{10,1... | collective-permute-start | bytes 6291464 | tf_op jit(solution)/shard_map/ppermute | solution.py:12
  40.9 4.7 fusion.43
  45.6 0.0 collective-permute-done.1
  45.6 0.0 copy-start.7
  45.6 5.0 tanh_add_fusion.5
  50.6 24.9 %collective-permute-start.2 = (f32[1024,512]{1,0:T(8,128)S(1)}, f32[1024,512]{1,0:T(8,128)S(1)}, u32[]{:S(2)}, u32[]{:S(2)}) collective-permute-start(f32[1024,512]{1,0:T(8,128)S(1)} %tanh_add_fusion.5), channel_id=1, source_target_pairs={{0,2},{1,3},{2,4},{3,5},{4,6},{5,7},{6,8},{7,9},{8,10},{9,11},{10,... | collective-permute-start | bytes 6291464 | tf_op jit(solution)/shard_map/ppermute | solution.py:12
  75.5 0.0 copy-done.7
  75.5 4.7 fusion.40
  80.2 39.2 %collective-permute-done.2 = f32[1024,512]{1,0:T(8,128)S(1)} collective-permute-done((f32[1024,512]{1,0:T(8,128)S(1)}, f32[1024,512]{1,0:T(8,128)S(1)}, u32[]{:S(2)}, u32[]{:S(2)}) %collective-permute-start.2) | collective-permute-done | bytes 2097184 | tf_op jit(solution)/shard_map/ppermute | solution.py:12
  119.4 0.0 copy-start.5
  119.4 5.1 tanh_add_fusion.4
  124.5 0.0 copy-done.5
  124.5 4.8 add_tanh_fusion.1
  129.3 0.0 all-gather.5.cloned.1.call-update
  129.3 0.4 all-gather.7.cloned.1.call-start
  129.8 177.0 %all-gather.5.cloned.1.call-done = f32[8192,512]{1,0:T(8,128)} async-done(((f32[1024,512]{1,0:T(8,128)}), f32[8192,512]{1,0:T(8,128)}) %all-gather.5.cloned.1.call-update) | async-done | bytes 16777232 | tf_op jit(solution)/shard_map/all_gather | solution.py:57
  306.8 9.4 %reduce_sum.18 = f32[1024,512]{1,0:T(8,128)} reduce(f32[8,1024,512]{2,1,0:T(8,128)} %bitcast.95, f32[]{:T(128)} %constant.4.clone.1), dimensions={0}, to_apply=%region_0.0 | reduce | flops 3670016 | bytes 18874372 | tf_op jit(solution)/shard_map/reduce_sum | solution.py:58
  316.2 0.0 copy-start.3
  316.2 5.5 fusion.16
  321.6 0.0 copy-done.3
  321.7 0.0 copy-start
  321.7 3.6 fusion.13
  325.2 0.0 copy-done
  325.2 3.7 tanh_add_fusion.3
  329.0 1.9 collective-permute-start.3
  330.9 0.1 slice.180
  330.9 4.7 fusion.33
  335.6 0.0 collective-permute-done.3
  335.6 0.1 slice.179
  335.7 5.0 tanh_add_fusion.2
  340.7 21.8 %collective-permute-start.4 = (f32[1024,512]{1,0:T(8,128)S(1)}, f32[1024,512]{1,0:T(8,128)S(1)}, u32[]{:S(2)}, u32[]{:S(2)}) collective-permute-start(f32[1024,512]{1,0:T(8,128)S(1)} %tanh_add_fusion.2), channel_id=1, source_target_pairs={{0,1},{1,2},{2,3},{3,4},{4,5},{5,6},{6,7},{7,8},{8,9},{9,10},{10,1... | collective-permute-start | bytes 6291464 | tf_op jit(solution)/shard_map/ppermute | solution.py:12
  362.5 4.7 fusion.30
  367.2 0.0 collective-permute-done.4
  367.2 4.9 tanh_add_fusion.1
  372.2 25.2 %collective-permute-start.5 = (f32[1024,512]{1,0:T(8,128)S(1)}, f32[1024,512]{1,0:T(8,128)S(1)}, u32[]{:S(2)}, u32[]{:S(2)}) collective-permute-start(f32[1024,512]{1,0:T(8,128)S(1)} %tanh_add_fusion.1), channel_id=1, source_target_pairs={{0,2},{1,3},{2,4},{3,5},{4,6},{5,7},{6,8},{7,9},{8,10},{9,11},{10,... | collective-permute-start | bytes 6291464 | tf_op jit(solution)/shard_map/ppermute | solution.py:12
  397.4 4.7 fusion.27
  402.1 39.1 %collective-permute-done.5 = f32[1024,512]{1,0:T(8,128)S(1)} collective-permute-done((f32[1024,512]{1,0:T(8,128)S(1)}, f32[1024,512]{1,0:T(8,128)S(1)}, u32[]{:S(2)}, u32[]{:S(2)}) %collective-permute-start.5) | collective-permute-done | bytes 2097184 | tf_op jit(solution)/shard_map/ppermute | solution.py:12
  441.2 0.0 copy-start.6
  441.2 5.1 tanh_add_fusion
  446.3 0.0 copy-done.6
  446.3 4.8 add_tanh_fusion
  451.1 0.0 all-gather.7.cloned.1.call-update
  451.1 174.1 %all-gather.7.cloned.1.call-done = f32[8192,512]{1,0:T(8,128)} async-done(((f32[1024,512]{1,0:T(8,128)}), f32[8192,512]{1,0:T(8,128)}) %all-gather.7.cloned.1.call-update) | async-done | bytes 16777232 | tf_op jit(solution)/shard_map/all_gather | solution.py:57
  625.2 9.7 %reduce_sum.19 = f32[1024,512]{1,0:T(8,128)} reduce(f32[8,1024,512]{2,1,0:T(8,128)} %bitcast.96, f32[]{:T(128)} %constant.4.clone.1), dimensions={0}, to_apply=%region_1.0 | reduce | flops 3670016 | bytes 18874372 | tf_op jit(solution)/shard_map/reduce_sum | solution.py:58
  634.8 0.0 copy-start.4
  634.8 5.5 fusion.11
  640.3 0.0 copy-done.4
  640.3 0.0 copy-start.1
  640.3 3.5 fusion.8
  643.9 0.0 copy-done.1
  643.9 5.0 add_bitcast_fusion
  (1 shorter events, 0.0 us)
Async XLA Ops:
  6.5 3.6 copy-start.2
  6.5 300.2 %all-gather.5.cloned.1.call-start = ((), (), s32[]{:S(2)}) async-start(), calls=%async_computation | async-start | bytes 18874368 | tf_op jit(solution)/shard_map/all_gather | solution.py:57
  6.5 8.3 %collective-permute-start = (f32[1024,512]{1,0:T(8,128)}, f32[1024,512]{1,0:T(8,128)S(1)}, u32[]{:S(2)}, u32[]{:S(2)}) collective-permute-start(f32[1024,512]{1,0:T(8,128)} %bitcast.97), channel_id=1, source_target_pairs={{0,1},{1,2},{2,3},{3,4},{4,5},{5,6},{6,7},{7,8},{8,9},{9,10},{10,1... | collective-permute-start | bytes 6291464 | tf_op jit(solution)/shard_map/ppermute | solution.py:12
  19.9 25.7 %collective-permute-start.1 = (f32[1024,512]{1,0:T(8,128)S(1)}, f32[1024,512]{1,0:T(8,128)S(1)}, u32[]{:S(2)}, u32[]{:S(2)}) collective-permute-start(f32[1024,512]{1,0:T(8,128)S(1)} %tanh_add_fusion.6), channel_id=1, source_target_pairs={{0,1},{1,2},{2,3},{3,4},{4,5},{5,6},{6,7},{7,8},{8,9},{9,10},{10,1... | collective-permute-start | bytes 6291464 | tf_op jit(solution)/shard_map/ppermute | solution.py:12
  45.6 29.9 %copy-start.7 = (f32[2,3,512]{2,0,1:T(2,128)S(1)}, f32[2,3,512]{2,0,1:T(2,128)}, u32[]{:S(2)}) copy-start(f32[2,3,512]{2,0,1:T(2,128)} %param.13) | copy-start | bytes 36868
  50.6 68.8 %collective-permute-start.2 = (f32[1024,512]{1,0:T(8,128)S(1)}, f32[1024,512]{1,0:T(8,128)S(1)}, u32[]{:S(2)}, u32[]{:S(2)}) collective-permute-start(f32[1024,512]{1,0:T(8,128)S(1)} %tanh_add_fusion.5), channel_id=1, source_target_pairs={{0,2},{1,3},{2,4},{3,5},{4,6},{5,7},{6,8},{7,9},{8,10},{9,11},{10,... | collective-permute-start | bytes 6291464 | tf_op jit(solution)/shard_map/ppermute | solution.py:12
  119.4 5.1 copy-start.5
  129.3 495.9 %all-gather.7.cloned.1.call-start = ((), (), s32[]{:S(2)}) async-start(), calls=%async_computation.1 | async-start | bytes 18874368 | tf_op jit(solution)/shard_map/all_gather | solution.py:57
  316.2 5.5 copy-start.3
  321.7 3.6 copy-start
  329.0 6.7 %collective-permute-start.3 = (f32[1024,512]{1,0:T(8,128)S(1)}, f32[1024,512]{1,0:T(8,128)S(1)}, u32[]{:S(2)}, u32[]{:S(2)}) collective-permute-start(f32[1024,512]{1,0:T(8,128)S(1)} %tanh_add_fusion.3), channel_id=1, source_target_pairs={{0,1},{1,2},{2,3},{3,4},{4,5},{5,6},{6,7},{7,8},{8,9},{9,10},{10,1... | collective-permute-start | bytes 6291464 | tf_op jit(solution)/shard_map/ppermute | solution.py:12
  340.7 26.5 %collective-permute-start.4 = (f32[1024,512]{1,0:T(8,128)S(1)}, f32[1024,512]{1,0:T(8,128)S(1)}, u32[]{:S(2)}, u32[]{:S(2)}) collective-permute-start(f32[1024,512]{1,0:T(8,128)S(1)} %tanh_add_fusion.2), channel_id=1, source_target_pairs={{0,1},{1,2},{2,3},{3,4},{4,5},{5,6},{6,7},{7,8},{8,9},{9,10},{10,1... | collective-permute-start | bytes 6291464 | tf_op jit(solution)/shard_map/ppermute | solution.py:12
  372.2 69.0 %collective-permute-start.5 = (f32[1024,512]{1,0:T(8,128)S(1)}, f32[1024,512]{1,0:T(8,128)S(1)}, u32[]{:S(2)}, u32[]{:S(2)}) collective-permute-start(f32[1024,512]{1,0:T(8,128)S(1)} %tanh_add_fusion.1), channel_id=1, source_target_pairs={{0,2},{1,3},{2,4},{3,5},{4,6},{5,7},{6,8},{7,9},{8,10},{9,11},{10,... | collective-permute-start | bytes 6291464 | tf_op jit(solution)/shard_map/ppermute | solution.py:12
  441.2 5.1 copy-start.6
  634.8 5.5 copy-start.4
  640.3 3.6 copy-start.1
Sparse Core Ops, SparseCore 0:
  129.4 177.2 all-gather.4
  451.2 173.9 all-gather.6
